TPU v7x, 128 devices: a whole 4x4x4 slice. The times are simulated.
128 devices in a mesh: grp: 4 (over x), sub: 32 (over z, y, core).
Axes of the slice: x: 4, y: 4, z: 4, core: 2. Of those that a mesh axis runs over, the one named last changes fastest.
Arguments:
- vectors: bfloat16 [128, 262144], P(None, ('grp', 'sub')), may hold values from -6 to 6
- geometry: bfloat16 [4, 262144], P(None, ('grp', 'sub')), may hold values from 0 to 4, as said below
- transfer: float32 [2, 4, 4, 512], P(None, 'grp'), may hold values from -6 to 6
Outputs:
- ortho_basis: float32 [128, 262144], P(None, ('grp', 'sub'))
- r_factor: float32 [128, 128], replicated
Inputs may be any that keep to these rules, and one draw needn't show every extreme that they name: `geometry`: rows 0 to 2 lie in the unit box, row 3 is positive and at least 0.25.
All inputs are finite; a program needn't handle non-finite values.
Results may differ from a plain program's by a relative error of at most 0.0065.
Values may be sent and summed in bfloat16 or wider, within the bound.
A program may use at most 128 MiB of HBM per device.

v0:
```python
import math
import jax
import jax.numpy as jnp
from jax import lax
from jax.sharding import PartitionSpec as P

KWAVE = 20.0
DELTA = 0.25
GOLDEN = math.pi * (3.0 - math.sqrt(5.0))


def extended(array, sides, width):
    for axis, dim in sides:
        size, length = (lax.axis_size(axis), array.shape[dim])
        up = [(i, (i + 1) % size) for i in range(size - 1)]
        down = [(j, i) for i, j in up]
        last = lax.slice_in_dim(array, length - width, length, axis=dim)
        leading = lax.slice_in_dim(array, 0, width, axis=dim)
        before = lax.ppermute(last, axis, up)
        after = lax.ppermute(leading, axis, down)
        array = jnp.concatenate([before, array, after], axis=dim)
    return array


def partner_2(block, axis, apart):
    count = lax.axis_size(axis)
    route = []
    for low in range(count):
        high = low | 1 << apart
        if high != low and high < count:
            route += [(low, high), (high, low)]
    return lax.ppermute(block, axis, route)


def kernel_tables(target, source, offsets):
    target_f = target.astype(jnp.float32)
    source_f = source.astype(jnp.float32)
    diff_x = target_f[0][None, :] - source_f[0][:, None] - offsets[:, None]
    diff_y = target_f[1][None, :] - source_f[1][:, None]
    diff_z = target_f[2][None, :] - source_f[2][:, None]
    dist_sq = diff_x * diff_x + diff_y * diff_y + diff_z * diff_z
    spread = source_f[3][:, None] / jnp.sqrt(dist_sq + DELTA * DELTA)
    phases = KWAVE * jnp.sqrt(dist_sq)
    return (
        (spread * jnp.cos(phases)).astype(jnp.bfloat16),
        (spread * jnp.sin(phases)).astype(jnp.bfloat16),
    )


def near_field(source_vec, source_geo, offsets, target_geo):
    half_cols = source_vec.shape[0] // 2
    panel_count = target_geo.shape[1]
    block_cols = min(512, panel_count)
    pieces = []
    for column in range(0, panel_count, block_cols):
        real_k, imag_k = kernel_tables(
            target_geo[:, column : column + block_cols], source_geo, offsets
        )
        part_a = jnp.dot(source_vec, real_k, preferred_element_type=jnp.float32)
        part_b = jnp.dot(source_vec, imag_k, preferred_element_type=jnp.float32)
        pieces.append(
            jnp.concatenate(
                (part_a[:half_cols] - part_b[half_cols:], part_a[half_cols:] + part_b[:half_cols]),
                0,
            )
        )
    return jnp.concatenate(pieces, 1)


def directions(dir_count):
    serial = jnp.arange(dir_count).astype(jnp.float32)
    height = 1.0 - (2.0 * serial + 1.0) / dir_count
    radius = jnp.sqrt(jnp.maximum(1.0 - height * height, 0.0))
    azimuth = serial * GOLDEN
    return (radius * jnp.cos(azimuth), radius * jnp.sin(azimuth), height)


def far_tables(geo, dir_count):
    points = geo.astype(jnp.float32)
    dir_x, dir_y, dir_z = directions(dir_count)
    phases = KWAVE * (
        dir_x[:, None] * points[0][None, :]
        + dir_y[:, None] * points[1][None, :]
        + dir_z[:, None] * points[2][None, :]
    )
    cos_table = jnp.cos(phases)
    sin_table = jnp.sin(phases)
    weight = points[3][None, :]
    return (
        (weight * cos_table).astype(jnp.bfloat16),
        (weight * sin_table).astype(jnp.bfloat16),
        cos_table.astype(jnp.bfloat16),
        sin_table.astype(jnp.bfloat16),
    )


def merge_pair(lower_fac, partner):
    contract = (((1,), (1,)), ((), ()))
    summed = lax.dot_general(
        lower_fac,
        lower_fac,
        contract,
        precision=lax.Precision.HIGHEST,
        preferred_element_type=jnp.float32,
    )
    summed = summed + lax.dot_general(
        partner,
        partner,
        contract,
        precision=lax.Precision.HIGHEST,
        preferred_element_type=jnp.float32,
    )
    return jnp.linalg.cholesky(summed)


def make_translate(tran_re, tran_im, half_cols):

    def translate(running, shard_piece, anchor):
        coef_re = tran_re[:, None, :]
        coef_im = tran_im[:, None, :]
        mom_re = shard_piece[:, :half_cols]
        mom_im = shard_piece[:, half_cols:]
        add_re = jnp.sum(coef_re * mom_re - coef_im * mom_im, axis=0)
        add_im = jnp.sum(coef_re * mom_im + coef_im * mom_re, axis=0)
        return jnp.concatenate((add_re, add_im), 0)

    return translate


def shards(vectors, geometry, transfer):
    half_cols = vectors.shape[0] // 2
    panel_count = vectors.shape[1]
    dir_count = transfer.shape[-1]
    sub_size = lax.axis_size("sub")
    grp_size = lax.axis_size("grp")
    contract = (((1,), (1,)), ((), ()))
    unit_row = jnp.ones((panel_count,), jnp.float32)
    joined = jnp.concatenate((vectors, geometry), 0)
    wide_rows = extended(joined, (("sub", 1),), panel_count)
    offsets = jnp.concatenate((-unit_row, 0.0 * unit_row, unit_row))
    near_part = near_field(
        wide_rows[: 2 * half_cols], wide_rows[2 * half_cols :], offsets, geometry
    )
    src_cos, src_sin, eval_cos, eval_sin = far_tables(geometry, dir_count)
    part_x = lax.dot_general(vectors, src_cos, contract, preferred_element_type=jnp.float32)
    part_z = lax.dot_general(vectors, src_sin, contract, preferred_element_type=jnp.float32)
    moment_scale = (panel_count * sub_size) ** (-0.5)
    moment = (
        jnp.concatenate(
            (part_x[:half_cols] + part_z[half_cols:], part_x[half_cols:] - part_z[:half_cols]), 0
        )
        * moment_scale
    )
    group_sum = lax.psum(moment, "sub")
    translate = make_translate(transfer[0, 0], transfer[1, 0], half_cols)
    local_exp = translate(
        jnp.zeros_like(group_sum),
        lax.all_gather(group_sum[None], "grp", axis=0, tiled=True),
        jnp.int32(0),
    )
    local_exp = local_exp.astype(jnp.bfloat16)
    part_a = jnp.dot(local_exp, eval_cos, preferred_element_type=jnp.float32)
    part_b = jnp.dot(local_exp, eval_sin, preferred_element_type=jnp.float32)
    far_part = jnp.concatenate(
        (part_a[:half_cols] - part_b[half_cols:], part_a[half_cols:] + part_b[:half_cols]), 0
    )
    near_scale = (3 * panel_count) ** (-0.5)
    far_scale = (dir_count * grp_size) ** (-0.5)
    applied = (
        0.5 * vectors.astype(jnp.float32) + near_scale * near_part + far_scale * far_part
    ).astype(jnp.bfloat16)
    inv_total = 1.0 / (panel_count * sub_size * grp_size)
    gram_mat = (
        lax.dot_general(applied, applied, contract, preferred_element_type=jnp.float32) * inv_total
    )
    lower_fac = jnp.linalg.cholesky(gram_mat)
    for level in range(sub_size.bit_length() - 1):
        partner = partner_2(lower_fac.astype(jnp.bfloat16), "sub", level).astype(lower_fac.dtype)
        lower_fac = merge_pair(lower_fac, partner)
    for level in range(grp_size.bit_length() - 1):
        partner = partner_2(lower_fac.astype(jnp.bfloat16), "grp", level).astype(lower_fac.dtype)
        lower_fac = merge_pair(lower_fac, partner)
    ortho_basis = lax.linalg.triangular_solve(
        lower_fac, applied.astype(jnp.float32), left_side=True, lower=True
    )
    return (ortho_basis, lower_fac.T)


def solution(mesh):
    in_specs = (P(None, ("grp", "sub")), P(None, ("grp", "sub")), P(None, "grp", None, None))
    out_specs = (P(None, ("grp", "sub")), P())
    return jax.shard_map(shards, mesh=mesh, in_specs=in_specs, out_specs=out_specs, check_vma=False)
```

profile of v0, /device:TPU:24, one launch (start us, length us, event | category | flops | bytes accessed | tf_op | source)
XLA Modules:
  0.0 758.0 jit_solution(7767568248212459756)
XLA Ops:
  9.0 2.1 collective-permute-start.1
  11.1 2.2 collective-permute-start
  14.3 18.9 %fusion.18 = f32[128,512]{1,0:T(8,128)S(1)} fusion(bf16[128,2048]{1,0:T(8,128)(2,1)} %param.4, f32[2048]{0:T(1024)S(1)} %bitcast.128, f32[512]{0:T(512)S(1)} %multiply_subtract_fusion, f32[2048]{0:T(1024)S(1)} %bitcast.124, f32[512]{0:T(512)S(1)} %get-tuple-element.55, f32[2048]{0:T(1024)S(1)} %bitcast.120, f32[512]{0:T(512)S(1)} %get-tuple-element.56, ...), kind=kOutput, calls=%fused_computation.40 | convolution fusion | flops 276824064 | bytes 825344 | tf_op jit(solution)/shard_map/dot_general | solution.py:146
  33.2 17.5 %fusion.19 = f32[128,512]{1,0:T(8,128)S(1)} fusion(bf16[128,2048]{1,0:T(8,128)(2,1)S(1)} %copy-done, f32[2048]{0:T(1024)S(1)} %bitcast.129, f32[512]{0:T(512)S(1)} %multiply_subtract_fusion, f32[2048]{0:T(1024)S(1)} %bitcast.125, f32[512]{0:T(512)S(1)} %get-tuple-element.55, f32[2048]{0:T(1024)S(1)} %bitcast.121, f32[512]{0:T(512)S(1)} %get-tuple-element.56, ...), kind=kOutput, calls=%fused_computation.41 | convolution fusion | flops 276824064 | bytes 825344 | tf_op jit(solution)/shard_map/dot_general | solution.py:145
  51.6 106.9 %all-reduce.2.cloned.1.call-done = f32[1,128,512]{2,1,0:T(8,128)} async-done(((f32[1,128,512]{2,1,0:T(8,128)}), f32[1,128,512]{2,1,0:T(8,128)}) %all-reduce.2.cloned.1.call-update) | async-done | bytes 262160 | tf_op jit(solution)/shard_map/psum | solution.py:154
  159.4 51.7 %fusion.5 = f32[128,512]{1,0:T(8,128)S(1)} fusion(f32[512]{0:T(512)S(1)} %bitcast.154, f32[512]{0:T(512)S(1)} %bitcast.156, f32[512]{0:T(512)S(1)} %bitcast.152, f32[6144]{0:T(1024)S(1)} %bitcast.96, f32[6144]{0:T(1024)S(1)} %bitcast.104, f32[6144]{0:T(1024)S(1)} %copy-done.3, f32[6144]{0:T(1024)S(1)} %bitcast.112, f32[6144]{0:T(1024)S(1)} %bitcast.88, ...), kind=kOutput, calls=%fused_computation.25 | convolution fusion | flops 849346560 | bytes 1964032 | tf_op jit(solution)/shard_map/dot_general | solution.py:60
  211.1 50.7 %fusion.4 = f32[128,512]{1,0:T(8,128)S(1)} fusion(f32[512]{0:T(512)S(1)} %bitcast.155, f32[512]{0:T(512)S(1)} %bitcast.157, f32[512]{0:T(512)S(1)} %bitcast.153, f32[6144]{0:T(1024)S(1)} %bitcast.97, f32[6144]{0:T(1024)S(1)} %bitcast.105, f32[6144]{0:T(1024)S(1)} %copy-done.3, f32[6144]{0:T(1024)S(1)} %bitcast.113, f32[6144]{0:T(1024)S(1)} %bitcast.89, ...), kind=kOutput, calls=%fused_computation.24 | convolution fusion | flops 849346560 | bytes 1964032 | tf_op jit(solution)/shard_map/dot_general | solution.py:59
  261.9 51.7 %fusion.3 = f32[128,512]{1,0:T(8,128)S(1)} fusion(f32[512]{0:T(512)S(1)} %bitcast.148, f32[512]{0:T(512)S(1)} %bitcast.146, f32[512]{0:T(512)S(1)} %bitcast.150, f32[6144]{0:T(1024)S(1)} %bitcast.98, f32[6144]{0:T(1024)S(1)} %bitcast.106, f32[6144]{0:T(1024)S(1)} %copy-done.3, f32[6144]{0:T(1024)S(1)} %bitcast.114, f32[6144]{0:T(1024)S(1)} %bitcast.90, ...), kind=kOutput, calls=%fused_computation.23 | convolution fusion | flops 849346560 | bytes 1964032 | tf_op jit(solution)/shard_map/dot_general | solution.py:60
  313.6 50.7 %fusion.2 = f32[128,512]{1,0:T(8,128)S(1)} fusion(f32[512]{0:T(512)S(1)} %bitcast.149, f32[512]{0:T(512)S(1)} %bitcast.147, f32[512]{0:T(512)S(1)} %bitcast.151, f32[6144]{0:T(1024)S(1)} %bitcast.99, f32[6144]{0:T(1024)S(1)} %bitcast.107, f32[6144]{0:T(1024)S(1)} %copy-done.3, f32[6144]{0:T(1024)S(1)} %bitcast.115, f32[6144]{0:T(1024)S(1)} %bitcast.91, ...), kind=kOutput, calls=%fused_computation.22 | convolution fusion | flops 849346560 | bytes 1964032 | tf_op jit(solution)/shard_map/dot_general | solution.py:59
  364.3 51.7 %fusion.1 = f32[128,512]{1,0:T(8,128)S(1)} fusion(f32[6144]{0:T(1024)S(1)} %bitcast.100, f32[512]{0:T(512)S(1)} %bitcast.142, f32[6144]{0:T(1024)S(1)} %bitcast.108, f32[512]{0:T(512)S(1)} %bitcast.144, f32[6144]{0:T(1024)S(1)} %copy-done.3, f32[6144]{0:T(1024)S(1)} %bitcast.116, f32[512]{0:T(512)S(1)} %bitcast.140, f32[6144]{0:T(1024)S(1)} %bitcast.92, ...), kind=kOutput, calls=%fused_computation.21 | convolution fusion | flops 849346560 | bytes 1964032 | tf_op jit(solution)/shard_map/dot_general | solution.py:60
  416.0 50.7 %fusion = f32[128,512]{1,0:T(8,128)S(1)} fusion(f32[6144]{0:T(1024)S(1)} %bitcast.101, f32[512]{0:T(512)S(1)} %bitcast.143, f32[6144]{0:T(1024)S(1)} %bitcast.109, f32[512]{0:T(512)S(1)} %bitcast.145, f32[6144]{0:T(1024)S(1)} %copy-done.3, f32[6144]{0:T(1024)S(1)} %bitcast.117, f32[512]{0:T(512)S(1)} %bitcast.141, f32[6144]{0:T(1024)S(1)} %bitcast.93, ...), kind=kOutput, calls=%fused_computation.20 | convolution fusion | flops 849346560 | bytes 1964032 | tf_op jit(solution)/shard_map/dot_general | solution.py:59
  466.8 51.1 %fusion.6 = f32[128,512]{1,0:T(8,128)S(1)} fusion(f32[512]{0:T(512)S(1)} %bitcast.136, f32[512]{0:T(512)S(1)} %bitcast.134, f32[512]{0:T(512)S(1)} %bitcast.138, f32[6144]{0:T(1024)S(1)} %bitcast.102, f32[6144]{0:T(1024)S(1)} %bitcast.110, f32[6144]{0:T(1024)S(1)} %copy-done.3, f32[6144]{0:T(1024)S(1)} %bitcast.118, f32[6144]{0:T(1024)S(1)} %bitcast.94, ...), kind=kOutput, calls=%fused_computation.26 | convolution fusion | flops 849346560 | bytes 1964032 | tf_op jit(solution)/shard_map/dot_general | solution.py:59
  517.9 51.7 %fusion.7 = f32[128,512]{1,0:T(8,128)S(1)} fusion(f32[512]{0:T(512)S(1)} %bitcast.137, f32[512]{0:T(512)S(1)} %bitcast.135, f32[512]{0:T(512)S(1)} %bitcast.139, f32[6144]{0:T(1024)S(1)} %bitcast.103, f32[6144]{0:T(1024)S(1)} %bitcast.111, f32[6144]{0:T(1024)S(1)} %copy-done.3, f32[6144]{0:T(1024)S(1)} %bitcast.119, f32[6144]{0:T(1024)S(1)} %bitcast.95, ...), kind=kOutput, calls=%fused_computation.27 | convolution fusion | flops 849346560 | bytes 1964032 | tf_op jit(solution)/shard_map/dot_general | solution.py:60
  571.1 14.7 %fusion.14 = f32[128,2048]{1,0:T(8,128)S(1)} fusion(f32[2048]{0:T(1024)S(1)} %bitcast.130, f32[512]{0:T(512)S(1)} %multiply_subtract_fusion, f32[2048]{0:T(1024)S(1)} %bitcast.126, f32[512]{0:T(512)S(1)} %get-tuple-element.55, f32[2048]{0:T(1024)S(1)} %bitcast.122, f32[512]{0:T(512)S(1)} %get-tuple-element.56, bf16[64,512]{1,0:T(8,128)(2,1)S(1)} %get-tuple-element.8, ...), kind=kOutput, calls=%fused_computation.36 | convolution fusion | flops 276037632 | bytes 1210368 | tf_op jit(solution)/shard_map/dot_general | solution.py:162
  585.7 14.8 %fusion.12 = f32[128,2048]{1,0:T(8,128)S(1)} fusion(f32[2048]{0:T(1024)S(1)} %bitcast.131, f32[512]{0:T(512)S(1)} %multiply_subtract_fusion, f32[2048]{0:T(1024)S(1)} %bitcast.127, f32[512]{0:T(512)S(1)} %get-tuple-element.55, f32[2048]{0:T(1024)S(1)} %bitcast.123, f32[512]{0:T(512)S(1)} %get-tuple-element.56, bf16[64,512]{1,0:T(8,128)(2,1)S(1)} %get-tuple-element.8, ...), kind=kOutput, calls=%fused_computation.35 | convolution fusion | flops 276037632 | bytes 1210368 | tf_op jit(solution)/shard_map/dot_general | solution.py:163
  601.4 11.7 %cholesky.134 = f32[128,128]{1,0:T(8,128)S(1)} custom-call(f32[128,128]{1,0:T(8,128)S(1)} %fusion.41), custom_call_target="Cholesky" | custom-call | tf_op jit(solution)/shard_map/jit(cholesky)/cholesky | solution.py:176
  616.4 11.7 %cholesky.145 = f32[128,128]{1,0:T(8,128)S(1)} custom-call(f32[128,128]{1,0:T(8,128)S(1)} %fusion.40), custom_call_target="Cholesky" | custom-call | tf_op jit(solution)/shard_map/jit(cholesky)/cholesky | solution.py:113
  630.5 3.0 collective-permute-done.3
  633.7 11.7 %cholesky.156 = f32[128,128]{1,0:T(8,128)S(1)} custom-call(f32[128,128]{1,0:T(8,128)S(1)} %fusion.39), custom_call_target="Cholesky" | custom-call | tf_op jit(solution)/shard_map/jit(cholesky)/cholesky | solution.py:113
  648.1 4.4 collective-permute-done.4
  652.7 11.7 %cholesky.167 = f32[128,128]{1,0:T(8,128)S(1)} custom-call(f32[128,128]{1,0:T(8,128)S(1)} %fusion.38), custom_call_target="Cholesky" | custom-call | tf_op jit(solution)/shard_map/jit(cholesky)/cholesky | solution.py:113
  666.8 3.0 collective-permute-done.5
  670.0 11.7 %cholesky.178 = f32[128,128]{1,0:T(8,128)S(1)} custom-call(f32[128,128]{1,0:T(8,128)S(1)} %fusion.37), custom_call_target="Cholesky" | custom-call | tf_op jit(solution)/shard_map/jit(cholesky)/cholesky | solution.py:113
  684.5 4.3 collective-permute-done.6
  689.1 11.7 %cholesky.189 = f32[128,128]{1,0:T(8,128)S(1)} custom-call(f32[128,128]{1,0:T(8,128)S(1)} %fusion.36), custom_call_target="Cholesky" | custom-call | tf_op jit(solution)/shard_map/jit(cholesky)/cholesky | solution.py:113
  702.1 1.5 collective-permute-start.7
  704.6 1.5 collective-permute-done.7
  706.4 11.7 %cholesky.200 = f32[128,128]{1,0:T(8,128)S(1)} custom-call(f32[128,128]{1,0:T(8,128)S(1)} %fusion.35), custom_call_target="Cholesky" | custom-call | tf_op jit(solution)/shard_map/jit(cholesky)/cholesky | solution.py:113
  719.5 3.3 collective-permute-start.8
  725.5 11.7 %cholesky.211 = f32[128,128]{1,0:T(8,128)S(1)} custom-call(f32[128,128]{1,0:T(8,128)S(1)} %fusion.34), custom_call_target="Cholesky" | custom-call | tf_op jit(solution)/shard_map/jit(cholesky)/cholesky | solution.py:113
  739.3 9.8 %custom-call.5 = f32[1,128,128]{1,2,0:T(8,128)S(1)} custom-call(f32[1,128,128]{2,1,0:T(8,128)S(1)} %get-tuple-element.26), custom_call_target="InvertDiagBlocksLowerTriangular" | custom-call | tf_op jit(solution)/shard_map/triangular_solve | solution.py:183
  749.1 1.6 fusion.32
  (99 shorter events, 29.8 us)
Async XLA Ops:
  7.2 151.4 %all-reduce.2.cloned.1.call-start = ((), (), s32[]{:S(2)}) async-start(), calls=%async_computation | async-start | bytes 524288 | tf_op jit(solution)/shard_map/psum | solution.py:154
  9.0 149.5 %collective-permute-start.1 = (bf16[132,2048]{1,0:T(8,128)(2,1)S(1)}, bf16[132,2048]{1,0:T(8,128)(2,1)S(1)}, u32[]{:S(2)}, u32[]{:S(2)}) collective-permute-start(bf16[132,2048]{1,0:T(8,128)(2,1)S(1)} %constant_dynamic-update-slice_fusion), channel_id=1, source_target_pairs={{1,0},{2,1},{3,2},{4,3},{5,4},{6,5},{7,6},{8,7},{9,8},{10,9},{11,1... | collective-permute-start | bytes 1622024 | tf_op jit(solution)/shard_map/ppermute | solution.py:20
  11.1 147.5 %collective-permute-start = (bf16[132,2048]{1,0:T(8,128)(2,1)S(1)}, bf16[132,2048]{1,0:T(8,128)(2,1)S(1)}, u32[]{:S(2)}, u32[]{:S(2)}) collective-permute-start(bf16[132,2048]{1,0:T(8,128)(2,1)S(1)} %constant_dynamic-update-slice_fusion), channel_id=1, source_target_pairs={{0,1},{1,2},{2,3},{3,4},{4,5},{5,6},{6,7},{7,8},{8,9},{9,10},{10,1... | collective-permute-start | bytes 1622024 | tf_op jit(solution)/shard_map/ppermute | solution.py:19
  14.3 18.9 %copy-start = (bf16[128,2048]{1,0:T(8,128)(2,1)S(1)}, bf16[128,2048]{1,0:T(8,128)(2,1)}, u32[]{:S(2)}) copy-start(bf16[128,2048]{1,0:T(8,128)(2,1)} %param.4) | copy-start | bytes 1572868
  33.2 18.3 %copy-start.1 = (bf16[4,2048]{1,0:T(4,128)(2,1)S(1)}, bf16[4,2048]{1,0:T(4,128)(2,1)}, u32[]{:S(2)}) copy-start(bf16[4,2048]{1,0:T(4,128)(2,1)} %param.5) | copy-start | bytes 49156
  50.7 0.9 copy-start.2
  51.5 518.2 %all-gather.2.cloned.1.call-start = ((), (), s32[]{:S(2)}) async-start(), calls=%async_computation.1 | async-start | bytes 1310720 | tf_op jit(solution)/shard_map/all_gather | solution.py:158
  158.7 0.7 copy-start.3
  614.4 1.7 collective-permute-start.2
  629.4 4.0 collective-permute-start.3
  646.8 5.7 collective-permute-start.4
  665.8 4.0 collective-permute-start.5
  683.1 5.7 collective-permute-start.6
  702.1 4.0 collective-permute-start.7
  719.5 5.8 collective-permute-start.8
Sparse Core Ops, SparseCore 0:
  51.6 106.8 all-reduce.1
  160.3 22.7 all-gather.1
where the time goes:
time: 767 us; the launch traced here: 758 us
  matrix products  485 us (63%)
  waiting for transfers between devices  125 us (16%)
  other arithmetic  117 us (15%)
  between operations  15 us (2%)
  starting transfers between devices  10.8 us (1%)
    dot_general x4, matrix products, near_field(): part_b = jnp.dot(source_vec, imag_k, preferred_element_type=jnp.float32)  207 us
    dot_general x4, matrix products, near_field(): part_a = jnp.dot(source_vec, real_k, preferred_element_type=jnp.float32)  203 us
    psum x1, waiting for transfers between devices, shards(): group_sum = lax.psum(moment, 'sub')  107 us
    another operation x21, other arithmetic, merge_pair(): return jnp.linalg.cholesky(summed)  86.7 us
    dot_general x1, matrix products, shards(): lax.dot_general(vectors, src_sin, contract, preferred_element_type=jnp.fl...  18.9 us
    ppermute x7, waiting for transfers between devices, partner_2(): return lax.ppermute(block, axis, route)  18 us
    dot_general x1, matrix products, shards(): lax.dot_general(vectors, src_cos, contract, preferred_element_type=jnp.fl...  17.5 us
  transfers between devices with their start and end apart: 11, of which 8 were waited for; matrix products, arithmetic and copies ran while one was open for 60% of the time, Pallas kernels for 0%

commit v1 on v0

--- a/solution.py
+++ b/solution.py
@@ -151,7 +151,7 @@
         )
         * moment_scale
     )
-    group_sum = lax.psum(moment, "sub")
+    group_sum = jnp.sum(lax.all_gather(moment, "sub"), axis=0)
     translate = make_translate(transfer[0, 0], transfer[1, 0], half_cols)
     local_exp = translate(
         jnp.zeros_like(group_sum),

time: 767 us -> 685 us (0.89)
  waiting for transfers between devices: 125 us -> 19.5 us
  starting transfers between devices: 10.8 us -> 22.9 us
  matrix products: 485 us -> 494 us
    psum x1 -> x0, waiting for transfers between devices: 107 us -> none  [shards(): group_sum = lax.psum(moment, 'sub')]
    ppermute x7, starting transfers between devices: 6.41 us -> 17.2 us  [partner_2(): return lax.ppermute(block, axis, route)]
    dot_general x1, matrix products: 17.5 us -> 26.3 us  [shards(): lax.dot_general(vectors, src_cos, contract, preferred_element_type=jnp.fl...]
  transfers between devices with their start and end apart: 11 -> 11, of which waited for: 8 -> 8; matrix products, arithmetic and copies ran while one was open for 60% -> 62% of each run, Pallas kernels for 0% -> 0%
where the time goes in v1:
time: 685 us; the launch traced here: 676 us
  matrix products  494 us (72%)
  other arithmetic  122 us (18%)
  starting transfers between devices  22.9 us (3%)
  waiting for transfers between devices  19.5 us (3%)
  between operations  15 us (2%)
    dot_general x4, matrix products, near_field(): part_b = jnp.dot(source_vec, imag_k, preferred_element_type=jnp.float32)  207 us
    dot_general x4, matrix products, near_field(): part_a = jnp.dot(source_vec, real_k, preferred_element_type=jnp.float32)  203 us
    another operation x21, other arithmetic, merge_pair(): return jnp.linalg.cholesky(summed)  86.7 us
    dot_general x1, matrix products, shards(): lax.dot_general(vectors, src_cos, contract, preferred_element_type=jnp.fl...  26.3 us
    dot_general x1, matrix products, shards(): lax.dot_general(vectors, src_sin, contract, preferred_element_type=jnp.fl...  18.7 us
    ppermute x7, starting transfers between devices, partner_2(): return lax.ppermute(block, axis, route)  17.2 us
    dot_general x1, matrix products, shards(): part_b = jnp.dot(local_exp, eval_sin, preferred_element_type=jnp.float32)  14.8 us
    dot_general x1, matrix products, shards(): part_a = jnp.dot(local_exp, eval_cos, preferred_element_type=jnp.float32)  14.7 us
  transfers between devices with their start and end apart: 11, of which 8 were waited for; matrix products, arithmetic and copies ran while one was open for 62% of the time, Pallas kernels for 0%

profile of v1, /device:TPU:24, one launch (start us, length us, event | category | flops | bytes accessed | tf_op | source)
XLA Modules:
  0.0 675.8 jit_solution(12890361794845709248)
XLA Ops:
  8.2 18.7 %fusion.18 = f32[128,512]{1,0:T(8,128)S(1)} fusion(bf16[128,2048]{1,0:T(8,128)(2,1)} %param.4, f32[2048]{0:T(1024)S(1)} %bitcast.132, f32[512]{0:T(512)S(1)} %multiply_subtract_fusion, f32[2048]{0:T(1024)S(1)} %bitcast.128, f32[512]{0:T(512)S(1)} %get-tuple-element.57, f32[2048]{0:T(1024)S(1)} %bitcast.124, f32[512]{0:T(512)S(1)} %get-tuple-element.58, ...), kind=kOutput, calls=%fused_computation.40 | convolution fusion | flops 276824064 | bytes 825344 | tf_op jit(solution)/shard_map/dot_general | solution.py:146
  27.0 26.3 %fusion.19 = f32[128,512]{1,0:T(8,128)S(1)} fusion(bf16[128,2048]{1,0:T(8,128)(2,1)S(1)} %copy-done, f32[2048]{0:T(1024)S(1)} %bitcast.133, f32[512]{0:T(512)S(1)} %multiply_subtract_fusion, f32[2048]{0:T(1024)S(1)} %bitcast.129, f32[512]{0:T(512)S(1)} %get-tuple-element.57, f32[2048]{0:T(1024)S(1)} %bitcast.125, f32[512]{0:T(512)S(1)} %get-tuple-element.58, ...), kind=kOutput, calls=%fused_computation.41 | convolution fusion | flops 276824064 | bytes 825344 | tf_op jit(solution)/shard_map/dot_general | solution.py:145
  54.2 1.9 collective-permute-start
  56.1 3.6 collective-permute-start.1
  59.8 5.2 collective-permute-done
  65.0 1.8 collective-permute-done.1
  67.1 51.1 %fusion = f32[128,512]{1,0:T(8,128)S(1)} fusion(f32[6144]{0:T(1024)S(1)} %bitcast.100, f32[512]{0:T(512)S(1)} %bitcast.158, f32[6144]{0:T(1024)S(1)} %bitcast.108, f32[512]{0:T(512)S(1)} %bitcast.160, f32[6144]{0:T(1024)S(1)} %copy-done.3, f32[6144]{0:T(1024)S(1)} %bitcast.116, f32[512]{0:T(512)S(1)} %bitcast.156, f32[6144]{0:T(1024)S(1)} %bitcast.92, ...), kind=kOutput, calls=%fused_computation.20 | convolution fusion | flops 849346560 | bytes 1964032 | tf_op jit(solution)/shard_map/dot_general | solution.py:59
  118.2 51.7 %fusion.1 = f32[128,512]{1,0:T(8,128)S(1)} fusion(f32[6144]{0:T(1024)S(1)} %bitcast.101, f32[512]{0:T(512)S(1)} %bitcast.159, f32[6144]{0:T(1024)S(1)} %bitcast.109, f32[512]{0:T(512)S(1)} %bitcast.161, f32[6144]{0:T(1024)S(1)} %copy-done.3, f32[6144]{0:T(1024)S(1)} %bitcast.117, f32[512]{0:T(512)S(1)} %bitcast.157, f32[6144]{0:T(1024)S(1)} %bitcast.93, ...), kind=kOutput, calls=%fused_computation.21 | convolution fusion | flops 849346560 | bytes 1964032 | tf_op jit(solution)/shard_map/dot_general | solution.py:60
  169.9 50.7 %fusion.2 = f32[128,512]{1,0:T(8,128)S(1)} fusion(f32[512]{0:T(512)S(1)} %bitcast.152, f32[512]{0:T(512)S(1)} %bitcast.150, f32[512]{0:T(512)S(1)} %bitcast.154, f32[6144]{0:T(1024)S(1)} %bitcast.102, f32[6144]{0:T(1024)S(1)} %bitcast.110, f32[6144]{0:T(1024)S(1)} %copy-done.3, f32[6144]{0:T(1024)S(1)} %bitcast.118, f32[6144]{0:T(1024)S(1)} %bitcast.94, ...), kind=kOutput, calls=%fused_computation.22 | convolution fusion | flops 849346560 | bytes 1964032 | tf_op jit(solution)/shard_map/dot_general | solution.py:59
  220.6 51.7 %fusion.3 = f32[128,512]{1,0:T(8,128)S(1)} fusion(f32[512]{0:T(512)S(1)} %bitcast.153, f32[512]{0:T(512)S(1)} %bitcast.151, f32[512]{0:T(512)S(1)} %bitcast.155, f32[6144]{0:T(1024)S(1)} %bitcast.103, f32[6144]{0:T(1024)S(1)} %bitcast.111, f32[6144]{0:T(1024)S(1)} %copy-done.3, f32[6144]{0:T(1024)S(1)} %bitcast.119, f32[6144]{0:T(1024)S(1)} %bitcast.95, ...), kind=kOutput, calls=%fused_computation.23 | convolution fusion | flops 849346560 | bytes 1964032 | tf_op jit(solution)/shard_map/dot_general | solution.py:60
  272.3 50.7 %fusion.4 = f32[128,512]{1,0:T(8,128)S(1)} fusion(f32[512]{0:T(512)S(1)} %bitcast.146, f32[512]{0:T(512)S(1)} %bitcast.148, f32[512]{0:T(512)S(1)} %bitcast.144, f32[6144]{0:T(1024)S(1)} %bitcast.104, f32[6144]{0:T(1024)S(1)} %bitcast.112, f32[6144]{0:T(1024)S(1)} %copy-done.3, f32[6144]{0:T(1024)S(1)} %bitcast.120, f32[6144]{0:T(1024)S(1)} %bitcast.96, ...), kind=kOutput, calls=%fused_computation.24 | convolution fusion | flops 849346560 | bytes 1964032 | tf_op jit(solution)/shard_map/dot_general | solution.py:59
  323.1 51.7 %fusion.5 = f32[128,512]{1,0:T(8,128)S(1)} fusion(f32[512]{0:T(512)S(1)} %bitcast.147, f32[512]{0:T(512)S(1)} %bitcast.149, f32[512]{0:T(512)S(1)} %bitcast.145, f32[6144]{0:T(1024)S(1)} %bitcast.105, f32[6144]{0:T(1024)S(1)} %bitcast.113, f32[6144]{0:T(1024)S(1)} %copy-done.3, f32[6144]{0:T(1024)S(1)} %bitcast.121, f32[6144]{0:T(1024)S(1)} %bitcast.97, ...), kind=kOutput, calls=%fused_computation.25 | convolution fusion | flops 849346560 | bytes 1964032 | tf_op jit(solution)/shard_map/dot_general | solution.py:60
  374.8 50.7 %fusion.6 = f32[128,512]{1,0:T(8,128)S(1)} fusion(f32[512]{0:T(512)S(1)} %bitcast.140, f32[512]{0:T(512)S(1)} %bitcast.138, f32[512]{0:T(512)S(1)} %bitcast.142, f32[6144]{0:T(1024)S(1)} %bitcast.106, f32[6144]{0:T(1024)S(1)} %bitcast.114, f32[6144]{0:T(1024)S(1)} %copy-done.4, f32[6144]{0:T(1024)S(1)} %bitcast.122, f32[6144]{0:T(1024)S(1)} %bitcast.98, ...), kind=kOutput, calls=%fused_computation.26 | convolution fusion | flops 849346560 | bytes 1964032 | tf_op jit(solution)/shard_map/dot_general | solution.py:59
  425.5 5.0 reduce_sum.27
  430.5 51.7 %fusion.7 = f32[128,512]{1,0:T(8,128)S(1)} fusion(f32[512]{0:T(512)S(1)} %bitcast.141, f32[512]{0:T(512)S(1)} %bitcast.139, f32[512]{0:T(512)S(1)} %bitcast.143, f32[6144]{0:T(1024)S(1)} %bitcast.107, f32[6144]{0:T(1024)S(1)} %bitcast.115, f32[6144]{0:T(1024)S(1)} %copy-done.4, f32[6144]{0:T(1024)S(1)} %bitcast.123, f32[6144]{0:T(1024)S(1)} %bitcast.99, ...), kind=kOutput, calls=%fused_computation.27 | convolution fusion | flops 849346560 | bytes 1964032 | tf_op jit(solution)/shard_map/dot_general | solution.py:60
  483.6 14.8 %fusion.12 = f32[128,2048]{1,0:T(8,128)S(1)} fusion(f32[2048]{0:T(1024)S(1)} %bitcast.134, f32[512]{0:T(512)S(1)} %multiply_subtract_fusion, f32[2048]{0:T(1024)S(1)} %bitcast.130, f32[512]{0:T(512)S(1)} %get-tuple-element.57, f32[2048]{0:T(1024)S(1)} %bitcast.126, f32[512]{0:T(512)S(1)} %get-tuple-element.58, bf16[64,512]{1,0:T(8,128)(2,1)S(1)} %get-tuple-element.10, ...), kind=kOutput, calls=%fused_computation.35 | convolution fusion | flops 276037632 | bytes 1210368 | tf_op jit(solution)/shard_map/dot_general | solution.py:163
  498.4 14.7 %fusion.14 = f32[128,2048]{1,0:T(8,128)S(1)} fusion(f32[2048]{0:T(1024)S(1)} %bitcast.135, f32[512]{0:T(512)S(1)} %multiply_subtract_fusion, f32[2048]{0:T(1024)S(1)} %bitcast.131, f32[512]{0:T(512)S(1)} %get-tuple-element.57, f32[2048]{0:T(1024)S(1)} %bitcast.127, f32[512]{0:T(512)S(1)} %get-tuple-element.58, bf16[64,512]{1,0:T(8,128)(2,1)S(1)} %get-tuple-element.10, ...), kind=kOutput, calls=%fused_computation.36 | convolution fusion | flops 276037632 | bytes 1210368 | tf_op jit(solution)/shard_map/dot_general | solution.py:162
  513.9 11.7 %cholesky.134 = f32[128,128]{1,0:T(8,128)S(1)} custom-call(f32[128,128]{1,0:T(8,128)S(1)} %fusion.42), custom_call_target="Cholesky" | custom-call | tf_op jit(solution)/shard_map/jit(cholesky)/cholesky | solution.py:176
  527.0 5.9 collective-permute-start.2
  534.1 11.7 %cholesky.145 = f32[128,128]{1,0:T(8,128)S(1)} custom-call(f32[128,128]{1,0:T(8,128)S(1)} %fusion.41), custom_call_target="Cholesky" | custom-call | tf_op jit(solution)/shard_map/jit(cholesky)/cholesky | solution.py:113
  548.2 3.0 collective-permute-done.3
  551.4 11.7 %cholesky.156 = f32[128,128]{1,0:T(8,128)S(1)} custom-call(f32[128,128]{1,0:T(8,128)S(1)} %fusion.40), custom_call_target="Cholesky" | custom-call | tf_op jit(solution)/shard_map/jit(cholesky)/cholesky | solution.py:113
  565.7 4.5 collective-permute-done.4
  570.4 11.7 %cholesky.167 = f32[128,128]{1,0:T(8,128)S(1)} custom-call(f32[128,128]{1,0:T(8,128)S(1)} %fusion.39), custom_call_target="Cholesky" | custom-call | tf_op jit(solution)/shard_map/jit(cholesky)/cholesky | solution.py:113
  583.5 2.0 collective-permute-start.5
  587.7 11.7 %cholesky.178 = f32[128,128]{1,0:T(8,128)S(1)} custom-call(f32[128,128]{1,0:T(8,128)S(1)} %fusion.38), custom_call_target="Cholesky" | custom-call | tf_op jit(solution)/shard_map/jit(cholesky)/cholesky | solution.py:113
  600.8 4.0 collective-permute-start.6
  606.9 11.7 %cholesky.189 = f32[128,128]{1,0:T(8,128)S(1)} custom-call(f32[128,128]{1,0:T(8,128)S(1)} %fusion.37), custom_call_target="Cholesky" | custom-call | tf_op jit(solution)/shard_map/jit(cholesky)/cholesky | solution.py:113
  624.2 11.7 %cholesky.200 = f32[128,128]{1,0:T(8,128)S(1)} custom-call(f32[128,128]{1,0:T(8,128)S(1)} %fusion.36), custom_call_target="Cholesky" | custom-call | tf_op jit(solution)/shard_map/jit(cholesky)/cholesky | solution.py:113
  637.3 3.4 collective-permute-start.8
  643.3 11.7 %cholesky.211 = f32[128,128]{1,0:T(8,128)S(1)} custom-call(f32[128,128]{1,0:T(8,128)S(1)} %fusion.35), custom_call_target="Cholesky" | custom-call | tf_op jit(solution)/shard_map/jit(cholesky)/cholesky | solution.py:113
  656.4 9.8 %custom-call.5 = f32[1,128,128]{1,2,0:T(8,128)S(1)} custom-call(f32[1,128,128]{2,1,0:T(8,128)S(1)} %get-tuple-element.28), custom_call_target="InvertDiagBlocksLowerTriangular" | custom-call | tf_op jit(solution)/shard_map/triangular_solve | solution.py:183
  (102 shorter events, 32.6 us)
Async XLA Ops:
  7.2 19.7 %copy-start = (bf16[128,2048]{1,0:T(8,128)(2,1)S(1)}, bf16[128,2048]{1,0:T(8,128)(2,1)}, u32[]{:S(2)}) copy-start(bf16[128,2048]{1,0:T(8,128)(2,1)} %param.4) | copy-start | bytes 1572868
  7.2 418.3 %all-gather.4.cloned.1.call-start = ((), (), s32[]{:S(2)}) async-start(), calls=%async_computation | async-start | bytes 8650752 | tf_op jit(solution)/shard_map/all_gather | solution.py:154
  26.9 27.2 %copy-start.1 = (bf16[4,2048]{1,0:T(4,128)(2,1)S(1)}, bf16[4,2048]{1,0:T(4,128)(2,1)}, u32[]{:S(2)}) copy-start(bf16[4,2048]{1,0:T(4,128)(2,1)} %param.5) | copy-start | bytes 49156
  26.9 32.9 %copy-start.2 = (f32[2,1,4,512]{3,2,1,0:T(4,128)S(1)}, f32[2,1,4,512]{3,2,1,0:T(4,128)}, u32[]{:S(2)}) copy-start(f32[2,1,4,512]{3,2,1,0:T(4,128)} %param.6) | copy-start | bytes 49156
  26.9 40.1 %copy-start.3 = (f32[6144]{0:T(1024)S(1)}, f32[6144]{0:T(1024)}, u32[]{:S(2)}) copy-start(f32[6144]{0:T(1024)} %constant.52.clone.1) | copy-start | bytes 73732
  54.1 428.2 %all-gather.6.cloned.1.call-start = ((), (), s32[]{:S(2)}) async-start(), calls=%async_computation.1 | async-start | bytes 1310720 | tf_op jit(solution)/shard_map/all_gather | solution.py:158
  54.2 10.9 %collective-permute-start = (bf16[132,2048]{1,0:T(8,128)(2,1)S(1)}, bf16[132,2048]{1,0:T(8,128)(2,1)S(1)}, u32[]{:S(2)}, u32[]{:S(2)}) collective-permute-start(bf16[132,2048]{1,0:T(8,128)(2,1)S(1)} %constant_dynamic-update-slice_fusion), channel_id=1, source_target_pairs={{0,1},{1,2},{2,3},{3,4},{4,5},{5,6},{6,7},{7,8},{8,9},{9,10},{10,1... | collective-permute-start | bytes 1622024 | tf_op jit(solution)/shard_map/ppermute | solution.py:19
  56.1 10.7 %collective-permute-start.1 = (bf16[132,2048]{1,0:T(8,128)(2,1)S(1)}, bf16[132,2048]{1,0:T(8,128)(2,1)S(1)}, u32[]{:S(2)}, u32[]{:S(2)}) collective-permute-start(bf16[132,2048]{1,0:T(8,128)(2,1)S(1)} %constant_dynamic-update-slice_fusion), channel_id=1, source_target_pairs={{1,0},{2,1},{3,2},{4,3},{5,4},{6,5},{7,6},{8,7},{9,8},{10,9},{11,1... | collective-permute-start | bytes 1622024 | tf_op jit(solution)/shard_map/ppermute | solution.py:20
  323.0 51.7 %copy-start.4 = (f32[6144]{0:T(1024)S(1)}, f32[6144]{0:T(1024)}, u32[]{:S(2)}) copy-start(f32[6144]{0:T(1024)} %constant.52.clone.1) | copy-start | bytes 73732
  527.0 6.9 %collective-permute-start.2 = (bf16[128,128]{1,0:T(8,128)(2,1)S(1)}, bf16[128,128]{1,0:T(8,128)(2,1)S(1)}, u32[]{:S(2)}, u32[]{:S(2)}) collective-permute-start(bf16[128,128]{1,0:T(8,128)(2,1)S(1)} %fusion.57), channel_id=1, source_target_pairs={{0,1},{1,0},{2,3},{3,2},{4,5},{5,4},{6,7},{7,6},{8,9},{9,8},{10,11... | collective-permute-start | bytes 98312 | tf_op jit(solution)/shard_map/ppermute | solution.py:32
  547.1 4.0 collective-permute-start.3
  564.5 5.7 collective-permute-start.4
  583.5 4.0 collective-permute-start.5
  600.8 5.8 collective-permute-start.6
  620.0 4.0 collective-permute-start.7
  637.3 5.8 collective-permute-start.8
Sparse Core Ops, SparseCore 0:
  54.2 55.6 all-gather.3
  430.6 30.6 all-gather.5
